TPU v7x, 32 devices: a whole 2x2x4 slice. The times are simulated.
32 devices in a mesh: dp: 8 (over y, x, core), mp: 4 (over z).
Axes of the slice: x: 2, y: 2, z: 4, core: 2. Of those that a mesh axis runs over, the one named last changes fastest.
Arguments:
- tokens: bfloat16 [2048, 1024], P('dp'), may hold values from -6 to 6
- norm_gain1: float32 [1024], replicated, may hold values from 0.25 to 1.75
- in_weight: bfloat16 [1024, 3, 1024], P(None, None, 'mp'), may hold values from -0.1875 to 0.1875
- conv_taps: float32 [3, 1024], P(None, 'mp'), may hold values from -3 to 3
- out_weight: bfloat16 [1024, 1024], P('mp'), may hold values from -0.1875 to 0.1875
- norm_gain2: float32 [1024], replicated, may hold values from 0.25 to 1.75
- gate_weight: bfloat16 [1024, 4608], P(None, 'mp'), may hold values from -0.1875 to 0.1875
- up_weight: bfloat16 [1024, 4608], P(None, 'mp'), may hold values from -0.1875 to 0.1875
- down_weight: bfloat16 [4608, 1024], P('mp'), may hold values from -0.09375 to 0.09375
- cotangent: bfloat16 [2048, 1024], P('dp'), may hold values from -6 to 6
Outputs:
- block_out: bfloat16 [2048, 1024], P('dp')
- input_grad: bfloat16 [2048, 1024], P('dp')
- grad_gain1: float32 [1024], replicated
- grad_in: float32 [1024, 3, 1024], P('dp', None, 'mp')
- grad_taps: float32 [3, 1024], P(None, 'mp')
- grad_out: float32 [1024, 1024], P('mp', 'dp')
- grad_gain2: float32 [1024], replicated
- grad_gate: float32 [1024, 4608], P('dp', 'mp')
- grad_up: float32 [1024, 4608], P('dp', 'mp')
- grad_down: float32 [4608, 1024], P('mp', 'dp')
All inputs are finite; a program needn't handle non-finite values.
Results may differ from a plain program's by a relative error of at most 0.0098.
Values sent between devices are 32-bit elements; how exact they have to be, the bound alone decides.
A program may use at most 128 MiB of HBM per device.

v0:
```python
import jax
import jax.numpy as jnp
from jax import lax
from jax.sharding import PartitionSpec as P

epsilon = 1e-05


def rms_forward(values, norm_gain):
    inverse = lax.rsqrt(jnp.mean(values * values, axis=-1, keepdims=True) + epsilon)
    unit = values * inverse
    return (unit, inverse, (unit * norm_gain).astype(jnp.bfloat16))


def rms_backward(grad_normed, unit, inverse, norm_gain):
    grad_gain = jnp.sum(grad_normed * unit, axis=0)
    scaled = grad_normed * norm_gain
    grad_values = inverse * (scaled - unit * jnp.mean(scaled * unit, axis=-1, keepdims=True))
    return (grad_values, grad_gain)


def lagged(values, offset):
    return jnp.pad(values, ((offset, 0), (0, 0)))[: values.shape[0]]


def leading(values, offset):
    return jnp.pad(values, ((0, offset), (0, 0)))[offset:]


def conv_forward(mixed, conv_taps):
    total = jnp.zeros(mixed.shape, jnp.float32)
    for offset in range(conv_taps.shape[0]):
        total = total + conv_taps[offset] * lagged(mixed, offset)
    return total


def conv_backward(grad_conv, mixed, conv_taps):
    grad_mixed = jnp.zeros(mixed.shape, jnp.float32)
    rows_list = []
    for offset in range(conv_taps.shape[0]):
        grad_mixed = grad_mixed + conv_taps[offset] * leading(grad_conv, offset)
        rows_list.append(jnp.sum(grad_conv * lagged(mixed, offset), axis=0))
    return (grad_mixed, jnp.stack(rows_list))


def body(
    tokens,
    norm_gain1,
    in_weight,
    conv_taps,
    out_weight,
    norm_gain2,
    gate_weight,
    up_weight,
    down_weight,
    cotangent,
):
    length = tokens.shape[0]
    width = tokens.shape[1]
    in_flat = in_weight.reshape(width, -1)
    streams = in_flat.shape[1]
    inputs = tokens.astype(jnp.float32)
    unit1, inverse1, normed1 = rms_forward(inputs, norm_gain1)
    proj = jnp.dot(normed1, in_flat, preferred_element_type=jnp.float32).reshape(length, 3, -1)
    gate_b = proj[:, 0]
    gate_c = proj[:, 1]
    stream_x = proj[:, 2]
    mixed = gate_b * stream_x
    conved = conv_forward(mixed, conv_taps)
    gated = (gate_c * conved).astype(jnp.bfloat16)
    branch = lax.psum(jnp.dot(gated, out_weight, preferred_element_type=jnp.float32), "mp")
    resid = inputs + branch
    unit2, inverse2, normed2 = rms_forward(resid, norm_gain2)
    gate_pre = jnp.dot(normed2, gate_weight, preferred_element_type=jnp.float32)
    up_pre = jnp.dot(normed2, up_weight, preferred_element_type=jnp.float32)
    sigmoid_gate = jax.nn.sigmoid(gate_pre)
    silu_gate = gate_pre * sigmoid_gate
    hidden = (silu_gate * up_pre).astype(jnp.bfloat16)
    ffn_out = lax.psum(jnp.dot(hidden, down_weight, preferred_element_type=jnp.float32), "mp")
    block_out = (resid + ffn_out).astype(jnp.bfloat16)
    grad_down = jnp.dot(hidden.T, cotangent, preferred_element_type=jnp.float32)
    grad_hidden = jnp.dot(cotangent, down_weight.T, preferred_element_type=jnp.float32)
    grad_gpre = (
        grad_hidden * up_pre * sigmoid_gate * (1.0 + gate_pre * (1.0 - sigmoid_gate))
    ).astype(jnp.bfloat16)
    grad_upre = (grad_hidden * silu_gate).astype(jnp.bfloat16)
    grad_gate = jnp.dot(normed2.T, grad_gpre, preferred_element_type=jnp.float32)
    grad_up = jnp.dot(normed2.T, grad_upre, preferred_element_type=jnp.float32)
    partial_norm2 = jnp.dot(grad_gpre, gate_weight.T, preferred_element_type=jnp.float32) + jnp.dot(
        grad_upre, up_weight.T, preferred_element_type=jnp.float32
    )
    grad_norm2 = lax.psum(partial_norm2, "mp")
    grad_from2, grad_gain2 = rms_backward(grad_norm2, unit2, inverse2, norm_gain2)
    grad_resid = cotangent.astype(jnp.float32) + grad_from2
    resid_bf = grad_resid.astype(jnp.bfloat16)
    grad_out = jnp.dot(gated.T, resid_bf, preferred_element_type=jnp.float32)
    grad_gated = jnp.dot(resid_bf, out_weight.T, preferred_element_type=jnp.float32)
    grad_c = grad_gated * conved
    grad_conv = grad_gated * gate_c
    grad_mixed, grad_taps = conv_backward(grad_conv, mixed, conv_taps)
    grad_proj = (
        jnp.stack([grad_mixed * stream_x, grad_c, grad_mixed * gate_b], axis=1)
        .astype(jnp.bfloat16)
        .reshape(length, streams)
    )
    grad_in = jnp.dot(normed1.T, grad_proj, preferred_element_type=jnp.float32)
    grad_norm1 = lax.psum(jnp.dot(grad_proj, in_flat.T, preferred_element_type=jnp.float32), "mp")
    grad_from1, grad_gain1 = rms_backward(grad_norm1, unit1, inverse1, norm_gain1)
    input_grad = (grad_resid + grad_from1).astype(jnp.bfloat16)
    summed_in, summed_out, summed_gate, summed_up, summed_down = (
        lax.psum_scatter(grad_in, "dp", scatter_dimension=0, tiled=True),
        lax.psum_scatter(grad_out, "dp", scatter_dimension=1, tiled=True),
        lax.psum_scatter(grad_gate, "dp", scatter_dimension=0, tiled=True),
        lax.psum_scatter(grad_up, "dp", scatter_dimension=0, tiled=True),
        lax.psum_scatter(grad_down, "dp", scatter_dimension=1, tiled=True),
    )
    total_gain1, total_taps, total_gain2 = lax.psum((grad_gain1, grad_taps, grad_gain2), "dp")
    return (
        block_out,
        input_grad,
        total_gain1,
        summed_in.reshape(summed_in.shape[0], 3, -1),
        total_taps,
        summed_out,
        total_gain2,
        summed_gate,
        summed_up,
        summed_down,
    )


def solution(mesh):
    in_specs = (
        P("dp", None),
        P(),
        P(None, None, "mp"),
        P(None, "mp"),
        P("mp", None),
        P(),
        P(None, "mp"),
        P(None, "mp"),
        P("mp", None),
        P("dp", None),
    )
    out_specs = (
        P("dp", None),
        P("dp", None),
        P(),
        P("dp", None, "mp"),
        P(None, "mp"),
        P("mp", "dp"),
        P(),
        P("dp", "mp"),
        P("dp", "mp"),
        P("mp", "dp"),
    )
    return jax.shard_map(body, mesh=mesh, in_specs=in_specs, out_specs=out_specs, check_vma=False)
```

profile of v0, /device:TPU:0, one launch (start us, length us, event | category | flops | bytes accessed | tf_op | source)
XLA Modules:
  0.0 491.8 jit_solution(12263484071148346959)
XLA Ops:
  7.3 2.7 copy.21
  10.0 0.2 fusion.14
  10.2 2.1 fusion
  12.4 0.8 copy-done.8
  13.2 0.8 multiply_convert_fusion.4
  14.0 1.3 fusion.32
  15.4 54.7 %all-reduce.10.cloned.1.call-done = f32[256,1024]{1,0:T(8,128)} async-done(((f32[256,1024]{1,0:T(8,128)}), f32[256,1024]{1,0:T(8,128)}) %all-reduce.10.cloned.1.call-update) | async-done | bytes 1048592 | tf_op jit(solution)/shard_map/psum | solution.py:71
  70.1 1.7 multiply_reduce_fusion.2
  71.9 0.2 multiply_convert_fusion.3
  72.0 0.2 copy-done.5
  72.3 0.9 fusion.33
  73.2 1.0 copy-done.4
  74.1 0.9 fusion.34
  75.0 0.2 copy-done.14
  75.2 2.1 multiply_convert_fusion
  77.3 0.9 fusion.36
  78.2 0.1 copy-done.10
  78.3 1.9 convolution_add_fusion
  80.3 2.9 fusion.35
  83.2 48.3 %all-reduce.12.cloned.1.call-done = f32[256,1024]{1,0:T(8,128)} async-done(((f32[256,1024]{1,0:T(8,128)}), f32[256,1024]{1,0:T(8,128)}) %all-reduce.12.cloned.1.call-update) | async-done | bytes 1048592 | tf_op jit(solution)/shard_map/psum | solution.py:92
  131.5 1.7 multiply_reduce_fusion
  133.3 0.3 multiply_add_fusion
  133.6 0.8 copy-done.9
  134.4 0.2 copy-done.17
  134.6 0.9 multiply_reduce_fusion.5
  135.8 0.5 copy-done.19
  136.3 0.1 copy-done.18
  136.5 1.6 convolution_bitcast_fusion
  138.2 1.8 maximum_convert_fusion
  139.9 1.9 copy.22
  141.8 3.6 fusion.26
  145.5 0.8 copy-done.21
  146.3 2.5 fusion.20
  148.9 4.3 fusion.37
  153.3 4.3 fusion.38
  157.7 4.3 fusion.39
  161.9 0.7 copy-done.25
  162.6 61.1 %all-reduce.14.cloned.1.call-done = (f32[256,1024]{1,0:T(8,128)}, f32[256,1024]{1,0:T(8,128)}) async-done(((f32[256,1024]{1,0:T(8,128)}, f32[256,1024]{1,0:T(8,128)}), (f32[256,1024]{1,0:T(8,128)}, f32[256,1024]{1,0:T(8,128)})) %all-reduce.14.cloned.1.call-update) | async-done | bytes 2097168 | tf_op jit(solution)/shard_map/psum | solution.py:79
  223.7 1.8 fusion.13
  225.5 23.6 %all-reduce.4 = (f32[1024]{0:T(1024)}, f32[3,256]{1,0:T(4,128)}, f32[1024]{0:T(1024)}) all-reduce(f32[1024]{0:T(1024)S(1)} %get-tuple-element.32, f32[3,256]{1,0:T(4,128)S(1)} %pad_maximum_fusion, f32[1024]{0:T(1024)S(1)} %get-tuple-element.30), channel_id=1, replica_groups=mesh['dp'=8,'mp'=4] {'dp'}, use_global_device_ids=true, to_apply=%region_9.10 | all-reduce | flops 2816 | bytes 22528 | tf_op jit(solution)/shard_map/psum | solution.py:117
  249.2 3.3 fusion.12
  252.5 19.7 %reduce-scatter.6.cloned.1.call-done = f32[128,768]{1,0:T(8,128)} async-done(((f32[1024,768]{1,0:T(8,128)}), f32[128,768]{1,0:T(8,128)}) %reduce-scatter.6.cloned.1.call-update) | async-done | bytes 393232 | tf_op jit(solution)/shard_map/reduce_scatter | solution.py:111
  272.1 1.1 copy.23
  273.3 0.9 copy.24
  274.2 37.5 %reduce-scatter.8.cloned.1.call-done = f32[256,128]{1,0:T(8,128)} async-done(((f32[256,1024]{1,0:T(8,128)}), f32[256,128]{1,0:T(8,128)}) %reduce-scatter.8.cloned.1.call-update) | async-done | bytes 131088 | tf_op jit(solution)/shard_map/reduce_scatter | solution.py:112
  311.7 57.7 %reduce-scatter.10.cloned.1.call-done = f32[128,1152]{1,0:T(8,128)} async-done(((f32[1024,1152]{1,0:T(8,128)}), f32[128,1152]{1,0:T(8,128)}) %reduce-scatter.10.cloned.1.call-update) | async-done | bytes 589840 | tf_op jit(solution)/shard_map/reduce_scatter | solution.py:113
  369.4 57.8 %reduce-scatter.12.cloned.1.call-done = f32[128,1152]{1,0:T(8,128)} async-done(((f32[1024,1152]{1,0:T(8,128)}), f32[128,1152]{1,0:T(8,128)}) %reduce-scatter.12.cloned.1.call-update) | async-done | bytes 589840 | tf_op jit(solution)/shard_map/reduce_scatter | solution.py:114
  427.2 57.7 %reduce-scatter.14.cloned.1.call-done = f32[1152,128]{1,0:T(8,128)} async-done(((f32[1152,1024]{1,0:T(8,128)}), f32[1152,128]{1,0:T(8,128)}) %reduce-scatter.14.cloned.1.call-update) | async-done | bytes 589840 | tf_op jit(solution)/shard_map/reduce_scatter | solution.py:115
  (71 shorter events, 0.9 us)
Async XLA Ops:
  7.2 67.8 %copy-start = (bf16[1152,1024]{1,0:T(8,128)(2,1)S(1)}, bf16[1152,1024]{1,0:T(8,128)(2,1)}, u32[]{:S(2)}) copy-start(bf16[1152,1024]{1,0:T(8,128)(2,1)} %param.18) | copy-start | bytes 7077892
  7.2 2.8 copy-start.3
  7.2 3.0 copy-start.24
  7.2 62.9 %all-reduce.10.cloned.1.call-start = ((), (), s32[]{:S(2)}) async-start(), calls=%async_computation.5 | async-start | bytes 2097152 | tf_op jit(solution)/shard_map/psum | solution.py:71
  10.0 2.4 copy-start.27
  10.2 3.8 copy-start.16
  12.3 0.9 copy-start.8
  12.4 3.0 copy-start.12
  14.0 1.4 copy-start.20
  14.0 57.9 %copy-start.23 = (f32[1024]{0:T(1024)S(1)}, f32[1024]{0:T(1024)}, u32[]{:S(2)}) copy-start(f32[1024]{0:T(1024)} %param.15) | copy-start | bytes 12292
  15.3 116.2 %all-reduce.12.cloned.1.call-start = ((), (), s32[]{:S(2)}) async-start(), calls=%async_computation.6 | async-start | bytes 2097152 | tf_op jit(solution)/shard_map/psum | solution.py:92
  70.1 2.1 copy-start.5
  72.3 0.9 copy-start.1
  72.3 1.9 copy-start.4
  74.1 1.0 copy-start.14
  77.3 0.9 copy-start.11
  77.3 1.0 copy-start.10
  80.2 143.5 %all-reduce.14.cloned.1.call-start = ((), (), s32[]{:S(2)}) async-start(), calls=%async_computation.12 | async-start | bytes 4194304 | tf_op jit(solution)/shard_map/psum | solution.py:79
  131.5 1.8 copy-start.7
  131.5 1.8 copy-start.15
  133.2 1.1 copy-start.9
  133.3 1.2 copy-start.13
  133.3 1.3 copy-start.17
  134.6 1.2 copy-start.2
  134.6 1.1 copy-start.22
  134.6 1.9 copy-start.6
  135.7 0.7 copy-start.19
  135.8 0.7 copy-start.18
  138.1 134.0 %reduce-scatter.6.cloned.1.call-start = ((), (), s32[]{:S(2)}) async-start(), calls=%async_computation.7 | async-start | bytes 3538944 | tf_op jit(solution)/shard_map/reduce_scatter | solution.py:111
  145.4 0.9 copy-start.21
  145.5 166.2 %reduce-scatter.8.cloned.1.call-start = ((), (), s32[]{:S(2)}) async-start(), calls=%async_computation.8 | async-start | bytes 1179648 | tf_op jit(solution)/shard_map/reduce_scatter | solution.py:112
  148.9 220.5 %reduce-scatter.10.cloned.1.call-start = ((), (), s32[]{:S(2)}) async-start(), calls=%async_computation.9 | async-start | bytes 5308416 | tf_op jit(solution)/shard_map/reduce_scatter | solution.py:113
  153.2 274.0 %reduce-scatter.12.cloned.1.call-start = ((), (), s32[]{:S(2)}) async-start(), calls=%async_computation.10 | async-start | bytes 5308416 | tf_op jit(solution)/shard_map/reduce_scatter | solution.py:114
  157.6 327.3 %reduce-scatter.14.cloned.1.call-start = ((), (), s32[]{:S(2)}) async-start(), calls=%async_computation.11 | async-start | bytes 5308416 | tf_op jit(solution)/shard_map/reduce_scatter | solution.py:115
  161.9 0.7 copy-start.25
  161.9 0.7 copy-start.26
Sparse Core Ops, SparseCore 0:
  15.5 54.6 all-reduce.9
  80.3 51.1 all-reduce.11
  138.2 85.4 all-reduce.13
  227.0 45.1 reduce-scatter.5
  275.7 35.9 reduce-scatter.7
  315.6 53.7 reduce-scatter.9
  373.4 53.7 reduce-scatter.11
  431.2 53.6 reduce-scatter.13
where the time goes:
time: 492 us
  waiting for transfers between devices  395 us (80%)
  matrix products  34.4 us (7%)
  blocking collectives  23.6 us (5%)
  between operations  14.4 us (3%)
  local copies, waits for them, and re-layouts  12.3 us (2%)
  other arithmetic  12 us (2%)
    psum x1, waiting for transfers between devices, body(): lax.psum(jnp.dot(hidden, down_weight, preferred_element_type=jnp.float32)...  61.1 us
    reduce_scatter x1, waiting for transfers between devices, body(): lax.psum_scatter(grad_up, 'dp', scatter_dimension=0, tiled=True)  57.8 us
    reduce_scatter x1, waiting for transfers between devices, body(): lax.psum_scatter(grad_down, 'dp', scatter_dimension=1, tiled=True)  57.7 us
    reduce_scatter x1, waiting for transfers between devices, body(): lax.psum_scatter(grad_gate, 'dp', scatter_dimension=0, tiled=True)  57.7 us
    psum x1, waiting for transfers between devices, body(): lax.psum(jnp.dot(gated, out_weight, preferred_element_type=jnp.float32),...  54.7 us
    psum x1, waiting for transfers between devices, body(): grad_norm2 = lax.psum(partial_norm2, 'mp')  48.3 us
    reduce_scatter x1, waiting for transfers between devices, body(): lax.psum_scatter(grad_out, 'dp', scatter_dimension=1, tiled=True)  37.5 us
    psum x1, blocking collectives, body(): lax.psum((grad_gain1, grad_taps, grad_gain2), 'dp')  23.6 us
  transfers between devices with their start and end apart: 8, of which 8 were waited for; matrix products, arithmetic and copies ran while one was open for 7% of the time, Pallas kernels for 0%

commit v1 on v0

--- a/solution.py
+++ b/solution.py
@@ -76,7 +76,8 @@
     sigmoid_gate = jax.nn.sigmoid(gate_pre)
     silu_gate = gate_pre * sigmoid_gate
     hidden = (silu_gate * up_pre).astype(jnp.bfloat16)
-    ffn_out = lax.psum(jnp.dot(hidden, down_weight, preferred_element_type=jnp.float32), "mp")
+    a0 = jnp.dot(hidden, down_weight, preferred_element_type=jnp.float32)
+    ffn_out = lax.all_gather(a0, axis_name="mp").sum(axis=0)
     block_out = (resid + ffn_out).astype(jnp.bfloat16)
     grad_down = jnp.dot(hidden.T, cotangent, preferred_element_type=jnp.float32)
     grad_hidden = jnp.dot(cotangent, down_weight.T, preferred_element_type=jnp.float32)

time: 492 us -> 545 us (1.11)
  waiting for transfers between devices: 395 us -> 441 us
  other arithmetic: 12 us -> 19.1 us
    all_gather x0 -> x1, waiting for transfers between devices: none -> 79.7 us  [body(): ffn_out = lax.all_gather(a0, axis_name='mp').sum(axis=0)]
    psum x1, waiting for transfers between devices: 61.1 us -> 27.1 us  [body(): lax.psum(jnp.dot(grad_proj, in_flat.T, preferred_element_type=jnp.float32...]
  transfers between devices with their start and end apart: 8 -> 9, of which waited for: 8 -> 9; matrix products, arithmetic and copies ran while one was open for 7% -> 6% of each run, Pallas kernels for 0% -> 0%
where the time goes in v1:
time: 545 us; the launch traced here: 544 us
  waiting for transfers between devices  441 us (81%)
  matrix products  33.8 us (6%)
  blocking collectives  24.1 us (4%)
  other arithmetic  19.1 us (4%)
  between operations  14.1 us (3%)
  local copies, waits for them, and re-layouts  11 us (2%)
    all_gather x1, waiting for transfers between devices, body(): ffn_out = lax.all_gather(a0, axis_name='mp').sum(axis=0)  79.7 us
    reduce_scatter x1, waiting for transfers between devices, body(): lax.psum_scatter(grad_up, 'dp', scatter_dimension=0, tiled=True)  57.8 us
    reduce_scatter x1, waiting for transfers between devices, body(): lax.psum_scatter(grad_gate, 'dp', scatter_dimension=0, tiled=True)  57.8 us
    reduce_scatter x1, waiting for transfers between devices, body(): lax.psum_scatter(grad_down, 'dp', scatter_dimension=1, tiled=True)  55.5 us
    psum x1, waiting for transfers between devices, body(): lax.psum(jnp.dot(gated, out_weight, preferred_element_type=jnp.float32),...  54.7 us
    psum x1, waiting for transfers between devices, body(): grad_norm2 = lax.psum(partial_norm2, 'mp')  48.3 us
    reduce_scatter x1, waiting for transfers between devices, body(): lax.psum_scatter(grad_out, 'dp', scatter_dimension=1, tiled=True)  39.8 us
    psum x1, waiting for transfers between devices, body(): lax.psum(jnp.dot(grad_proj, in_flat.T, preferred_element_type=jnp.float32...  27.1 us
  transfers between devices with their start and end apart: 9, of which 9 were waited for; matrix products, arithmetic and copies ran while one was open for 6% of the time, Pallas kernels for 0%

profile of v1, /device:TPU:0, one launch (start us, length us, event | category | flops | bytes accessed | tf_op | source)
XLA Modules:
  0.0 543.7 jit_solution(18265309840009982418)
XLA Ops:
  7.3 1.4 fusion.14
  8.6 0.8 fusion.31
  9.5 2.6 copy.21
  12.0 2.1 fusion
  14.2 0.9 copy-done.7
  15.1 0.8 multiply_convert_fusion.4
  15.9 1.3 fusion.32
  17.3 54.7 %all-reduce.9.cloned.1.call-done = f32[256,1024]{1,0:T(8,128)} async-done(((f32[256,1024]{1,0:T(8,128)}), f32[256,1024]{1,0:T(8,128)}) %all-reduce.9.cloned.1.call-update) | async-done | bytes 1048592 | tf_op jit(solution)/shard_map/psum | solution.py:71
  72.0 1.6 multiply_reduce_fusion.2
  73.6 0.2 multiply_convert_fusion.3
  73.8 0.2 copy-done.4
  74.0 0.9 fusion.34
  74.9 0.8 copy-done.5
  75.6 0.9 fusion.33
  76.5 0.2 copy-done.15
  76.7 2.1 multiply_convert_fusion
  78.8 0.9 fusion.36
  79.8 1.9 convolution_add_fusion
  81.8 2.9 fusion.35
  84.8 48.3 %all-reduce.11.cloned.1.call-done = f32[256,1024]{1,0:T(8,128)} async-done(((f32[256,1024]{1,0:T(8,128)}), f32[256,1024]{1,0:T(8,128)}) %all-reduce.11.cloned.1.call-update) | async-done | bytes 1048592 | tf_op jit(solution)/shard_map/psum | solution.py:93
  133.0 1.9 multiply_reduce_fusion
  134.9 79.7 %all-gather.3.cloned.1.call-done = f32[1024,1024]{1,0:T(8,128)} async-done(((f32[256,1024]{1,0:T(8,128)}), f32[1024,1024]{1,0:T(8,128)}) %all-gather.3.cloned.1.call-update) | async-done | bytes 4194320 | tf_op jit(solution)/shard_map/all_gather | solution.py:80
  214.6 3.7 reduce_sum.92
  218.3 3.3 multiply_add_fusion
  221.6 1.0 multiply_reduce_fusion.5
  222.8 0.5 copy-done.17
  223.3 0.1 copy-done.16
  223.5 1.6 convolution_bitcast_fusion
  225.2 1.8 maximum_convert_fusion
  226.9 1.9 copy.22
  228.8 3.3 fusion.26
  232.2 4.3 fusion.39
  236.6 4.1 fusion.38
  240.7 0.2 reduce-scatter.10.cloned.1.call-start
  241.0 4.1 fusion.37
  245.2 0.8 copy-done.19
  246.0 2.5 fusion.20
  248.6 27.1 %all-reduce.13.cloned.1.call-done = f32[256,1024]{1,0:T(8,128)} async-done(((f32[256,1024]{1,0:T(8,128)}), f32[256,1024]{1,0:T(8,128)}) %all-reduce.13.cloned.1.call-update) | async-done | bytes 1048592 | tf_op jit(solution)/shard_map/psum | solution.py:108
  275.6 1.7 fusion.13
  277.3 24.1 %all-reduce.4 = (f32[1024]{0:T(1024)}, f32[3,256]{1,0:T(4,128)}, f32[1024]{0:T(1024)}) all-reduce(f32[1024]{0:T(1024)S(1)} %get-tuple-element.32, f32[3,256]{1,0:T(4,128)S(1)} %pad_maximum_fusion, f32[1024]{0:T(1024)S(1)} %get-tuple-element.30), channel_id=1, replica_groups=mesh['dp'=8,'mp'=4] {'dp'}, use_global_device_ids=true, to_apply=%region_9.10 | all-reduce | flops 2816 | bytes 22528 | tf_op jit(solution)/shard_map/psum | solution.py:118
  301.4 2.6 fusion.12
  304.0 20.2 %reduce-scatter.6.cloned.1.call-done = f32[128,768]{1,0:T(8,128)} async-done(((f32[1024,768]{1,0:T(8,128)}), f32[128,768]{1,0:T(8,128)}) %reduce-scatter.6.cloned.1.call-update) | async-done | bytes 393232 | tf_op jit(solution)/shard_map/reduce_scatter | solution.py:112
  324.2 1.1 copy.23
  325.4 0.9 copy.24
  326.3 55.5 %reduce-scatter.14.cloned.1.call-done = f32[1152,128]{1,0:T(8,128)} async-done(((f32[1152,1024]{1,0:T(8,128)}), f32[1152,128]{1,0:T(8,128)}) %reduce-scatter.14.cloned.1.call-update) | async-done | bytes 589840 | tf_op jit(solution)/shard_map/reduce_scatter | solution.py:116
  381.8 57.8 %reduce-scatter.12.cloned.1.call-done = f32[128,1152]{1,0:T(8,128)} async-done(((f32[1024,1152]{1,0:T(8,128)}), f32[128,1152]{1,0:T(8,128)}) %reduce-scatter.12.cloned.1.call-update) | async-done | bytes 589840 | tf_op jit(solution)/shard_map/reduce_scatter | solution.py:115
  439.6 57.8 %reduce-scatter.10.cloned.1.call-done = f32[128,1152]{1,0:T(8,128)} async-done(((f32[1024,1152]{1,0:T(8,128)}), f32[128,1152]{1,0:T(8,128)}) %reduce-scatter.10.cloned.1.call-update) | async-done | bytes 589840 | tf_op jit(solution)/shard_map/reduce_scatter | solution.py:114
  497.5 39.8 %reduce-scatter.8.cloned.1.call-done = f32[256,128]{1,0:T(8,128)} async-done(((f32[256,1024]{1,0:T(8,128)}), f32[256,128]{1,0:T(8,128)}) %reduce-scatter.8.cloned.1.call-update) | async-done | bytes 131088 | tf_op jit(solution)/shard_map/reduce_scatter | solution.py:113
  (69 shorter events, 0.9 us)
Async XLA Ops:
  7.2 69.3 %copy-start = (bf16[1152,1024]{1,0:T(8,128)(2,1)S(1)}, bf16[1152,1024]{1,0:T(8,128)(2,1)}, u32[]{:S(2)}) copy-start(bf16[1152,1024]{1,0:T(8,128)(2,1)} %param.18) | copy-start | bytes 7077892
  7.2 4.8 copy-start.3
  7.2 4.8 copy-start.22
  7.2 64.8 %all-reduce.9.cloned.1.call-start = ((), (), s32[]{:S(2)}) async-start(), calls=%async_computation.5 | async-start | bytes 2097152 | tf_op jit(solution)/shard_map/psum | solution.py:71
  12.0 3.8 copy-start.13
  14.1 0.9 copy-start.7
  14.2 59.4 %copy-start.11 = (f32[256,256]{1,0:T(8,128)}, f32[256,256]{1,0:T(8,128)S(1)}, u32[]{:S(2)}) copy-start(f32[256,256]{1,0:T(8,128)S(1)} %fusion.25) | copy-start | bytes 786436
  15.9 57.7 %copy-start.18 = (bf16[256,256]{1,0:T(8,128)(2,1)}, bf16[256,256]{1,0:T(8,128)(2,1)S(1)}, u32[]{:S(2)}) copy-start(bf16[256,256]{1,0:T(8,128)(2,1)S(1)} %get-tuple-element.45) | copy-start | bytes 393220
  15.9 57.8 %copy-start.21 = (f32[1024]{0:T(1024)S(1)}, f32[1024]{0:T(1024)}, u32[]{:S(2)}) copy-start(f32[1024]{0:T(1024)} %param.15) | copy-start | bytes 12292
  17.2 115.8 %all-reduce.11.cloned.1.call-start = ((), (), s32[]{:S(2)}) async-start(), calls=%async_computation.6 | async-start | bytes 2097152 | tf_op jit(solution)/shard_map/psum | solution.py:93
  72.0 2.0 copy-start.4
  73.6 1.2 copy-start.1
  74.0 1.7 copy-start.5
  75.6 1.0 copy-start.15
  78.8 0.9 copy-start.10
  78.8 1.0 copy-start.9
  81.7 132.9 %all-gather.3.cloned.1.call-start = ((), (), s32[]{:S(2)}) async-start(), calls=%async_computation.13 | async-start | bytes 5242880 | tf_op jit(solution)/shard_map/all_gather | solution.py:80
  84.7 190.9 %all-reduce.13.cloned.1.call-start = ((), (), s32[]{:S(2)}) async-start(), calls=%async_computation.7 | async-start | bytes 2097152 | tf_op jit(solution)/shard_map/psum | solution.py:108
  218.3 3.3 copy-start.8
  218.3 3.3 copy-start.12
  218.3 3.3 copy-start.14
  221.6 1.2 copy-start.2
  221.6 1.1 copy-start.20
  221.6 1.8 copy-start.6
  222.7 0.7 copy-start.17
  222.8 0.7 copy-start.16
  225.1 99.1 %reduce-scatter.6.cloned.1.call-start = ((), (), s32[]{:S(2)}) async-start(), calls=%async_computation.8 | async-start | bytes 3538944 | tf_op jit(solution)/shard_map/reduce_scatter | solution.py:112
  232.2 149.6 %reduce-scatter.14.cloned.1.call-start = ((), (), s32[]{:S(2)}) async-start(), calls=%async_computation.12 | async-start | bytes 5308416 | tf_op jit(solution)/shard_map/reduce_scatter | solution.py:116
  236.5 203.1 %reduce-scatter.12.cloned.1.call-start = ((), (), s32[]{:S(2)}) async-start(), calls=%async_computation.11 | async-start | bytes 5308416 | tf_op jit(solution)/shard_map/reduce_scatter | solution.py:115
  240.7 256.7 %reduce-scatter.10.cloned.1.call-start = ((), (), s32[]{:S(2)}) async-start(), calls=%async_computation.10 | async-start | bytes 5308416 | tf_op jit(solution)/shard_map/reduce_scatter | solution.py:114
  245.1 0.9 copy-start.19
  245.1 3.4 copy-start.23
  245.1 3.4 copy-start.24
  245.1 292.1 %reduce-scatter.8.cloned.1.call-start = ((), (), s32[]{:S(2)}) async-start(), calls=%async_computation.9 | async-start | bytes 1179648 | tf_op jit(solution)/shard_map/reduce_scatter | solution.py:113
Sparse Core Ops, SparseCore 0:
  17.3 54.6 all-reduce.8
  81.8 51.1 all-reduce.10
  134.6 79.9 all-gather.2
  225.2 50.3 all-reduce.12
  278.9 45.3 reduce-scatter.5
  328.1 53.6 reduce-scatter.13
  385.8 53.7 reduce-scatter.11
  443.6 53.7 reduce-scatter.9
  501.2 35.9 reduce-scatter.7
